TPU v7x, 32 devices: a whole 2x2x4 slice. The times are simulated.
32 devices in a mesh: dp: 2 (over y), expert: 4 (over x, core), tensor: 4 (over z).
Axes of the slice: x: 2, y: 2, z: 4, core: 2. Of those that a mesh axis runs over, the one named last changes fastest.
Arguments:
- hidden_states: bfloat16 [256, 4096], P(('dp', 'expert'), 'tensor'), may hold values from -6 to 6
- chosen_experts: int32 [256, 2], P(('dp', 'expert')), may hold values from 0 to 3, all different within a row; in each aligned block of 32 rows (0 to 31, 32 to 63, ...) at most 16 rows name the same one
- choice_weights: float32 [256, 2], P(('dp', 'expert')), may hold values from 0.2 to 1
- gate_proj: bfloat16 [4, 4096, 8192], P('expert', None, ('dp', 'tensor')), may hold values from -0.09375 to 0.09375
- up_proj: bfloat16 [4, 4096, 8192], P('expert', None, ('dp', 'tensor')), may hold values from -0.09375 to 0.09375
- down_proj: bfloat16 [4, 8192, 4096], P('expert', 'dp', 'tensor'), may hold values from -0.0625 to 0.0625
Outputs:
- moe_output: bfloat16 [256, 4096], P(('dp', 'expert'), 'tensor')
Inputs may be any that keep to these rules, and one draw needn't show every extreme that they name: `chosen_experts`: each row names 2 different experts; among the 32 rows of one device no expert is named more than 16 times, a bound that some block reaches.
All inputs are finite; a program needn't handle non-finite values.
Results may differ from a plain program's by a relative error of at most 0.0058.
Values may be sent and summed in bfloat16 or wider, within the bound.
A program may use at most 64 MiB of HBM per device.

v0:
```python
import jax
import jax.numpy as jnp
from jax import lax
from jax.sharding import PartitionSpec as P

CAP = 16


def slot_tables(chosen_experts, experts, capacity):
    flat_ids = chosen_experts.reshape(-1)
    onehot = (flat_ids[:, None] == jnp.arange(experts, dtype=jnp.int32)[None, :]).astype(jnp.int32)
    before = jnp.cumsum(onehot, axis=0) - onehot
    position = jnp.sum(before * onehot, axis=1)
    return (flat_ids * capacity + position).reshape(chosen_experts.shape)


def body(hidden_states, chosen_experts, choice_weights, gate_proj, up_proj, down_proj):
    experts = lax.axis_size("expert")
    token_count = hidden_states.shape[0]
    feat_width = hidden_states.shape[1]
    slot_count = experts * CAP
    target = slot_tables(chosen_experts, experts, CAP)
    slot_ids = jnp.arange(slot_count, dtype=jnp.int32)
    placing = jnp.zeros((slot_count, token_count), jnp.float32)
    weights_table = jnp.zeros((token_count, slot_count), jnp.float32)
    for column in range(target.shape[1]):
        placing = placing + (slot_ids[:, None] == target[None, :, column]).astype(jnp.float32)
        weights_table = weights_table + jnp.where(
            target[:, column][:, None] == slot_ids[None, :],
            choice_weights[:, column][:, None],
            jnp.float32(0.0),
        )
    packed = jnp.dot(
        placing.astype(jnp.bfloat16), hidden_states, preferred_element_type=jnp.float32
    )
    packed = packed.astype(jnp.bfloat16).reshape(experts, CAP, feat_width)
    arrived = lax.all_to_all(packed, "expert", split_axis=0, concat_axis=0, tiled=True).reshape(
        slot_count, feat_width
    )
    gate_weights = gate_proj[0]
    up_weights = up_proj[0]
    down_weights = down_proj[0]
    features = lax.all_gather(arrived, "tensor", axis=1, tiled=True)
    shards = lax.all_gather(features, "dp", axis=0, tiled=True)
    gate_part = jnp.dot(shards, gate_weights, preferred_element_type=jnp.float32)
    up_part = jnp.dot(shards, up_weights, preferred_element_type=jnp.float32)
    activated = (jax.nn.silu(gate_part) * up_part).astype(jnp.bfloat16)
    unit_rows = lax.all_gather(activated, "tensor", axis=1, tiled=True)
    summed = lax.psum_scatter(
        jnp.dot(unit_rows, down_weights, preferred_element_type=jnp.float32),
        "dp",
        scatter_dimension=0,
        tiled=True,
    )
    outgoing = summed.astype(jnp.bfloat16).reshape(experts, CAP, feat_width)
    returned = lax.all_to_all(outgoing, "expert", split_axis=0, concat_axis=0, tiled=True).reshape(
        slot_count, feat_width
    )
    combined = jnp.dot(
        weights_table,
        returned.astype(jnp.float32),
        precision=lax.Precision.HIGHEST,
        preferred_element_type=jnp.float32,
    )
    return combined.astype(jnp.bfloat16)


def solution(mesh):
    in_specs = (
        P(("dp", "expert"), "tensor"),
        P(("dp", "expert"), None),
        P(("dp", "expert"), None),
        P("expert", None, ("dp", "tensor")),
        P("expert", None, ("dp", "tensor")),
        P("expert", "dp", "tensor"),
    )
    out_specs = P(("dp", "expert"), "tensor")
    return jax.shard_map(body, mesh=mesh, in_specs=in_specs, out_specs=out_specs, check_vma=False)
```

profile of v0, /device:TPU:0, one launch (start us, length us, event | category | flops | bytes accessed | tf_op | source)
XLA Modules:
  0.0 131.8 jit_solution(14651087666373031079)
XLA Ops:
  6.5 0.8 copy.13
  7.3 0.1 eq.71
  7.4 0.1 fusion.12
  7.5 0.1 reduce_window_sum.11
  7.6 0.2 select_reduce_fusion
  7.8 0.1 reduce_sum.12
  7.9 0.1 copy.14
  8.0 0.7 multiply_add_fusion
  8.7 0.2 convolution_convert_fusion
  8.9 8.6 %all_to_all.10 = bf16[4,16,1024]{2,1,0:T(8,128)(2,1)S(1)} all-to-all(bf16[4,16,1024]{2,1,0:T(8,128)(2,1)S(1)} %bitcast.31), channel_id=1, replica_groups=mesh['dp'=2,'expert'=4,'tensor'=4] {'expert'}, dimensions={0} | all-to-all | bytes 262144 | tf_op jit(solution)/shard_map/all_to_all | solution.py:37
  17.5 16.2 %all_gather.9 = bf16[64,4096]{1,0:T(8,128)(2,1)} all-gather(bf16[64,1024]{1,0:T(8,128)(2,1)S(1)} %bitcast.30), channel_id=1, replica_groups=mesh['dp'=2,'expert'=4,'tensor'=4] {'tensor'}, dimensions={1}, use_global_device_ids=true | all-gather | bytes 655360 | tf_op jit(solution)/shard_map/all_gather | solution.py:43
  33.8 0.0 all-gather.3.cloned.1.call-update
  33.8 0.0 all-gather.5.cloned.1.call-start
  33.8 22.4 %all-gather.3.cloned.1.call-done = bf16[128,4096]{1,0:T(8,128)(2,1)} async-done(((bf16[64,4096]{1,0:T(8,128)(2,1)}), bf16[128,4096]{1,0:T(8,128)(2,1)}) %all-gather.3.cloned.1.call-update) | async-done | bytes 1048592 | tf_op jit(solution)/shard_map/all_gather | solution.py:44
  56.2 5.0 %fusion.4 = f32[128,1024]{1,0:T(8,128)S(1)} fusion(bf16[128,4096]{1,0:T(8,128)(2,1)} %all-gather.3.cloned.1.call-done, bf16[1,4096,1024]{2,1,0:T(8,128)(2,1)} %param.9), kind=kOutput, calls=%fused_computation.4 | convolution fusion | flops 1073741824 | bytes 9961472 | tf_op jit(solution)/shard_map/dot_general | solution.py:45
  61.2 5.5 %fusion.9 = bf16[128,1024]{1,0:T(8,128)(2,1)} fusion(bf16[128,4096]{1,0:T(8,128)(2,1)S(1)} %copy-done.1, bf16[1,4096,1024]{2,1,0:T(8,128)(2,1)} %param.10, f32[128,1024]{1,0:T(8,128)S(1)} %fusion.4), kind=kOutput, calls=%fused_computation.7 | convolution fusion | flops 1074528256 | bytes 10223616 | tf_op jit(solution)/shard_map/dot_general | solution.py:46
  66.8 0.0 reduce-scatter.2.cloned.1.call-start
  66.8 28.0 %all-gather.5.cloned.1.call-done = bf16[128,4096]{1,0:T(8,128)(2,1)} async-done(((bf16[128,1024]{1,0:T(8,128)(2,1)}), bf16[128,4096]{1,0:T(8,128)(2,1)}) %all-gather.5.cloned.1.call-update) | async-done | bytes 1048592 | tf_op jit(solution)/shard_map/all_gather | solution.py:48
  94.8 5.8 %fusion = f32[128,1024]{1,0:T(8,128)} fusion(bf16[128,4096]{1,0:T(8,128)(2,1)} %all-gather.5.cloned.1.call-done, bf16[1,4096,1024]{2,1,0:T(8,128)(2,1)} %param.11), kind=kOutput, calls=%fused_computation | convolution fusion | flops 1073741824 | bytes 9961472 | tf_op jit(solution)/shard_map/dot_general | solution.py:50
  100.7 14.2 %reduce-scatter.2.cloned.1.call-done = f32[64,1024]{1,0:T(8,128)} async-done(((f32[128,1024]{1,0:T(8,128)}), f32[64,1024]{1,0:T(8,128)}) %reduce-scatter.2.cloned.1.call-update) | async-done | bytes 262160 | tf_op jit(solution)/shard_map/reduce_scatter | solution.py:49
  114.9 1.6 %convert_element_type.31 = bf16[64,1024]{1,0:T(8,128)(2,1)} convert(f32[64,1024]{1,0:T(8,128)} %reduce-scatter.2.cloned.1.call-done) | non-fusion elementwise | flops 65536 | bytes 393216 | tf_op jit(solution)/shard_map/convert_element_type | solution.py:55
  116.5 3.3 %all-to-all-start.1 = ((bf16[4,16,1024]{2,1,0:T(8,128)(2,1)}), bf16[4,16,1024]{2,1,0:T(8,128)(2,1)S(1)}, u32[]{:S(2)}, u32[]{:S(2)}) async-start(bf16[4,16,1024]{2,1,0:T(8,128)(2,1)} %bitcast.9), calls=%async_computation.2 | async-start | bytes 262144 | tf_op jit(solution)/shard_map/all_to_all | solution.py:56
  119.8 4.6 %all-to-all-done.1 = bf16[4,16,1024]{2,1,0:T(8,128)(2,1)S(1)} async-done(((bf16[4,16,1024]{2,1,0:T(8,128)(2,1)}), bf16[4,16,1024]{2,1,0:T(8,128)(2,1)S(1)}, u32[]{:S(2)}, u32[]{:S(2)}) %all-to-all-start.1) | async-done | bytes 131104 | tf_op jit(solution)/shard_map/all_to_all | solution.py:56
  124.4 0.9 convolution_convert_fusion.1
  (11 shorter events, 0.1 us)
Async XLA Ops:
  6.5 2.2 %copy-start = (bf16[32,1024]{1,0:T(8,128)(2,1)S(1)}, bf16[32,1024]{1,0:T(8,128)(2,1)}, u32[]{:S(2)}) copy-start(bf16[32,1024]{1,0:T(8,128)(2,1)} %param.6) | copy-start | bytes 196612
  6.5 49.7 %all-gather.3.cloned.1.call-start = ((), (), s32[]{:S(2)}) async-start(), calls=%async_computation.3 | async-start | bytes 1572864 | tf_op jit(solution)/shard_map/all_gather | solution.py:44
  33.8 61.1 %all-gather.5.cloned.1.call-start = ((), (), s32[]{:S(2)}) async-start(), calls=%async_computation.4 | async-start | bytes 1310720 | tf_op jit(solution)/shard_map/all_gather | solution.py:48
  56.2 5.0 %copy-start.1 = (bf16[128,4096]{1,0:T(8,128)(2,1)S(1)}, bf16[128,4096]{1,0:T(8,128)(2,1)}, u32[]{:S(2)}) copy-start(bf16[128,4096]{1,0:T(8,128)(2,1)} %all-gather.3.cloned.1.call-done) | copy-start | bytes 3145732
  66.8 53.1 %copy-start.2 = (f32[32,2]{0,1:T(2,128)S(1)}, f32[32,2]{0,1:T(2,128)}, u32[]{:S(2)}) copy-start(f32[32,2]{0,1:T(2,128)} %param.8) | copy-start | bytes 772
  66.8 48.1 %reduce-scatter.2.cloned.1.call-start = ((), (), s32[]{:S(2)}) async-start(), calls=%async_computation.5 | async-start | bytes 786432 | tf_op jit(solution)/shard_map/reduce_scatter | solution.py:49
  116.5 7.9 %all-to-all-start.1 = ((bf16[4,16,1024]{2,1,0:T(8,128)(2,1)}), bf16[4,16,1024]{2,1,0:T(8,128)(2,1)S(1)}, u32[]{:S(2)}, u32[]{:S(2)}) async-start(bf16[4,16,1024]{2,1,0:T(8,128)(2,1)} %bitcast.9), calls=%async_computation.2 | async-start | bytes 262144 | tf_op jit(solution)/shard_map/all_to_all | solution.py:56
Sparse Core Ops, SparseCore 0:
  33.9 22.2 all-gather.2
  66.9 27.9 all-gather.4
  100.8 14.0 reduce-scatter.1
where the time goes:
time: 132 us
  waiting for transfers between devices  69.2 us (52%)
  blocking collectives  24.9 us (19%)
  matrix products  17.4 us (13%)
  between operations  13.2 us (10%)
  starting transfers between devices  3.41 us (3%)
  other arithmetic  2.66 us (2%)
    all_gather x1, waiting for transfers between devices, body(): unit_rows = lax.all_gather(activated, 'tensor', axis=1, tiled=True)  28 us
    all_gather x1, waiting for transfers between devices, body(): shards = lax.all_gather(features, 'dp', axis=0, tiled=True)  22.4 us
    all_gather x1, blocking collectives, body(): features = lax.all_gather(arrived, 'tensor', axis=1, tiled=True)  16.2 us
    reduce_scatter x1, waiting for transfers between devices, body(): lax.psum_scatter(jnp.dot(unit_rows, down_weights, preferred_element_type=...  14.2 us
    all_to_all x1, blocking collectives, body(): lax.all_to_all(packed, 'expert', split_axis=0, concat_axis=0, tiled=True)  8.64 us
    dot_general x1, matrix products, body(): jnp.dot(unit_rows, down_weights, preferred_element_type=jnp.float32)  5.79 us
    dot_general x1, matrix products, body(): up_part = jnp.dot(shards, up_weights, preferred_element_type=jnp.float32)  5.48 us
    dot_general x1, matrix products, body(): jnp.dot(shards, gate_weights, preferred_element_type=jnp.float32)  5.03 us
  transfers between devices with their start and end apart: 4, of which 4 were waited for; matrix products, arithmetic and copies ran while one was open for 0% of the time, Pallas kernels for 0%

commit v1 on v0

v1 whole, which is shorter than its diff:
```python
import functools

import jax
import jax.numpy as jnp
from jax import lax
from jax.experimental import pallas as pl
from jax.experimental.pallas import tpu as pltpu
from jax.sharding import PartitionSpec as P

CAP = 16
HOP = 2
CHUNKS = 2
MESH = pl.DeviceIdType.MESH


def kernel(
    nd, ne, nt,
    hidden_ref, ids_ref, weights_ref, gate_hbm, up_hbm, down_hbm, out_ref,
    packed, feats, acts, gate_w, up_w, down_w, gate_acc, up_acc, down_acc,
    outgoing, returned, table,
    w_sem, a2a_send, a2a_recv, z_send, z_recv, y_send, y_recv, ret_send, ret_recv,
):
    d, e, t = lax.axis_index("dp"), lax.axis_index("expert"), lax.axis_index("tensor")
    tokens, width = hidden_ref.shape
    slots = ne * CAP
    units = gate_w.shape[2]
    part = ne // CHUNKS
    tile_u = min(256, units)
    tile_f = min(256, width)

    def weight_copies(s):
        rows_f = pl.ds(pl.multiple_of(s * width, width), width)
        rows_u = pl.ds(pl.multiple_of(s * units, units), units)
        return (
            pltpu.make_async_copy(gate_hbm.at[0, rows_f], gate_w.at[s], w_sem.at[0, s]),
            pltpu.make_async_copy(up_hbm.at[0, rows_f], up_w.at[s], w_sem.at[1, s]),
            pltpu.make_async_copy(down_hbm.at[0, rows_u], down_w.at[s], w_sem.at[2, s]),
        )

    order = [0]
    for k in range(1, nt):
        order.append((k + 1) // 2 if k % 2 else nt - k // 2)
    for k in order:
        for copy in weight_copies(lax.rem(t + k, nt))[:2]:
            copy.start()
    for k in order:
        weight_copies(lax.rem(t + k, nt))[2].start()

    barrier = pltpu.get_barrier_semaphore()
    for j in range(nd):
        for k in range(ne):
            if j or k:
                pl.semaphore_signal(
                    barrier, inc=1, device_id_type=MESH,
                    device_id=(lax.rem(d + j, nd), lax.rem(e + k, ne), t),
                )
    for k in range(1, nt):
        pl.semaphore_signal(
            barrier, inc=1, device_id=(d, e, lax.rem(t + k, nt)), device_id_type=MESH
        )

    slot = lax.broadcasted_iota(jnp.int32, (tokens, slots), 1)
    slot_expert = lax.shift_right_logical(slot, CAP.bit_length() - 1)
    slot_place = slot - slot_expert * CAP
    named = jnp.zeros((tokens, slots), jnp.float32)
    weighted = jnp.zeros((tokens, slots), jnp.float32)
    for column in range(ids_ref.shape[1]):
        match = ids_ref[:, column : column + 1] == slot_expert
        named = jnp.where(match, 1.0, named)
        weighted = jnp.where(match, weights_ref[:, column : column + 1], weighted)
    earlier = lax.broadcasted_iota(jnp.int32, (tokens, tokens), 0) > (
        lax.broadcasted_iota(jnp.int32, (tokens, tokens), 1)
    )
    position = jnp.dot(
        jnp.where(earlier, 1.0, 0.0).astype(jnp.bfloat16),
        named.astype(jnp.bfloat16),
        preferred_element_type=jnp.float32,
    )
    placing = jnp.where(position == slot_place.astype(jnp.float32), named, 0.0)
    weighted = weighted * placing
    high = weighted.astype(jnp.bfloat16)
    rest = weighted - high.astype(jnp.float32)
    middle = rest.astype(jnp.bfloat16)
    table[0:tokens, :] = high
    table[tokens : 2 * tokens, :] = middle
    table[2 * tokens :, :] = (rest - middle.astype(jnp.float32)).astype(jnp.bfloat16)
    packed[...] = (
        lax.dot_general(
            placing.astype(jnp.bfloat16), hidden_ref[...], (((0,), (0,)), ((), ())),
            preferred_element_type=jnp.float32,
        )
        .astype(jnp.bfloat16)
        .reshape(ne, CAP, width)
    )
    pl.semaphore_wait(barrier, nd * ne + nt - 2)

    def a2a_copy(k):
        return pltpu.make_async_remote_copy(
            src_ref=packed.at[lax.rem(e + k, ne)],
            dst_ref=feats.at[d, t, e],
            send_sem=a2a_send.at[k],
            recv_sem=a2a_recv.at[e],
            device_id=(d, lax.rem(e + k, ne), t),
            device_id_type=MESH,
        )

    for k in range(1, ne):
        a2a_copy(k).start()
    feats[d, t, e] = packed[e]
    for k in range(1, ne):
        source = lax.rem(e + k, ne)
        pltpu.make_async_remote_copy(
            src_ref=packed.at[0],
            dst_ref=feats.at[d, t, source],
            send_sem=a2a_send.at[k],
            recv_sem=a2a_recv.at[source],
            device_id=(d, source, t),
            device_id_type=MESH,
        ).wait_recv()

    def z_copy(phase, ref, s, c, side, dist, hop):
        block = ref.at[s, pl.ds(c * part, part)]
        return pltpu.make_async_remote_copy(
            src_ref=block,
            dst_ref=block,
            send_sem=z_send.at[phase, c, side, dist // HOP, hop - 1],
            recv_sem=z_recv.at[phase, c, s],
            device_id=(d, e, t + hop * (1 - 2 * side)),
            device_id_type=MESH,
        )

    def for_targets(side, dist, act):
        step = 1 - 2 * side
        s = t - step * dist
        for hop in range(1, HOP + 1):
            to = t + step * hop

            @pl.when((s >= 0) & (s < nt) & (to >= 0) & (to < nt))
            def _():
                act(s, hop)

    def z_forward(phase, ref, side, dist, c):
        if dist % HOP == 0:
            for_targets(
                side, dist,
                lambda s, hop: z_copy(phase, ref, s, c, side, dist, hop).start(),
            )

    def z_drain(phase, ref):
        for c in range(CHUNKS):
            for side in range(2):
                for dist in range(0, nt, HOP):
                    for_targets(
                        side, dist,
                        lambda s, hop: z_copy(phase, ref, s, c, side, dist, hop).wait_send(),
                    )

    def z_arrive(phase, ref, s, c):
        z_copy(phase, ref, s, c, 0, 0, 1).wait_recv()

    def y_copy(j, b, s, c):
        block = feats.at[b, s, pl.ds(c * part, part)]
        return pltpu.make_async_remote_copy(
            src_ref=block,
            dst_ref=block,
            send_sem=y_send.at[j, s, c],
            recv_sem=y_recv.at[b, s, c],
            device_id=(lax.rem(d + j, nd), e, t),
            device_id_type=MESH,
        )

    def y_spread(s, c):
        for j in range(1, nd):
            y_copy(j, d, s, c).start()

    def gate_up(b, s, first):
        @pl.loop(0, units // tile_u)
        def _(i):
            columns = pl.ds(pl.multiple_of(i * tile_u, tile_u), tile_u)
            rows = feats[b, s].reshape(slots, width)
            gate = jnp.dot(rows, gate_w[s, :, columns], preferred_element_type=jnp.float32)
            up = jnp.dot(rows, up_w[s, :, columns], preferred_element_type=jnp.float32)
            if first is True:
                gate_acc[:, columns] = gate
                up_acc[:, columns] = up
            else:
                gate_acc[:, columns] += gate
                up_acc[:, columns] += up

    def activate(b):
        @pl.loop(0, units // tile_u)
        def _(i):
            columns = pl.ds(pl.multiple_of(i * tile_u, tile_u), tile_u)
            gate = gate_acc[:, columns]
            value = gate / (1.0 + jnp.exp(-gate)) * up_acc[:, columns]
            acts[b, t, :, :, columns] = value.astype(jnp.bfloat16).reshape(ne, CAP, tile_u)

    def down(b, s, first):
        @pl.loop(0, width // tile_f)
        def _(i):
            columns = pl.ds(pl.multiple_of(i * tile_f, tile_f), tile_f)
            rows = acts[b, s].reshape(slots, units)
            value = jnp.dot(rows, down_w[s, :, columns], preferred_element_type=jnp.float32)
            if first:
                down_acc[:, columns] = value
            else:
                down_acc[:, columns] += value

    def at_distance(dist, act):
        for side in range(2):
            s = t - (1 - 2 * side) * dist

            @pl.when((s >= 0) & (s < nt))
            def _():
                act(side, s)

    own = feats.at[d]
    for c in range(CHUNKS):
        z_forward(0, own, 0, 0, c)
        z_forward(0, own, 1, 0, c)
        y_spread(t, c)

    def weights_arrive(s):
        for copy in weight_copies(s)[:2]:
            copy.wait()

    weights_arrive(t)
    gate_up(d, t, True)
    for dist in range(1, nt):
        def take(side, s):
            for c in range(CHUNKS):
                z_arrive(0, own, s, c)
                z_forward(0, own, side, dist, c)
                y_spread(s, c)

        def use(side, s):
            weights_arrive(s)
            gate_up(d, s, False)

        at_distance(dist, take)
        at_distance(dist, use)
    activate(d)
    for c in range(CHUNKS):
        for side in range(2):
            z_forward(1, acts.at[d], side, 0, c)

    def other_rows(j, carry):
        b = lax.rem(d + j, nd)

        def arrive(s):
            for c in range(CHUNKS):
                y_copy(j, b, s, c).wait_recv()

        arrive(t)
        gate_up(b, t, True)

        def shard(k, carry):
            s = lax.rem(t + k, nt)
            arrive(s)
            gate_up(b, s, False)
            return carry

        lax.fori_loop(1, nt, shard, 0)
        activate(b)
        for c in range(CHUNKS):
            for side in range(2):
                z_forward(1 + j, acts.at[b], side, 0, c)
        return carry

    lax.fori_loop(1, nd, other_rows, 0)

    for k in range(nt):
        weight_copies(lax.rem(t + k, nt))[2].wait()

    def return_copy(j, b, k):
        to = lax.rem(e + k, ne)
        return pltpu.make_async_remote_copy(
            src_ref=outgoing.at[b, to],
            dst_ref=returned.at[d, e],
            send_sem=ret_send.at[j, k],
            recv_sem=ret_recv.at[d, e],
            device_id=(b, to, t),
            device_id_type=MESH,
        )

    def finish(j, carry):
        b = lax.rem(d + j, nd)
        ref = acts.at[b]
        down(b, t, True)
        for dist in range(1, nt):
            def take(side, s):
                for c in range(CHUNKS):
                    z_arrive(1 + j, ref, s, c)
                    z_forward(1 + j, ref, side, dist, c)

            at_distance(dist, take)
            at_distance(dist, lambda side, s: down(b, s, False))
        outgoing[b] = down_acc[...].astype(jnp.bfloat16).reshape(ne, CAP, width)
        for k in range(1, ne):
            return_copy(j, b, k).start()

        @pl.when(j == 0)
        def _():
            returned[d, e] = outgoing[d, e]

        @pl.when(j > 0)
        def _():
            return_copy(j, b, 0).start()

        return carry

    lax.fori_loop(0, nd, finish, 0)

    for j in range(nd):
        for k in range(ne):
            if j or k:
                b, source = lax.rem(d + j, nd), lax.rem(e + k, ne)
                pltpu.make_async_remote_copy(
                    src_ref=outgoing.at[0, 0],
                    dst_ref=returned.at[b, source],
                    send_sem=ret_send.at[j, k],
                    recv_sem=ret_recv.at[b, source],
                    device_id=(b, source, t),
                    device_id_type=MESH,
                ).wait_recv()
    total = jnp.zeros((table.shape[0], width), jnp.float32)
    for b in range(nd):
        total += jnp.dot(
            table[...], returned[b].reshape(slots, width), preferred_element_type=jnp.float32
        )
    out_ref[...] = (
        total[0:tokens] + total[tokens : 2 * tokens] + total[2 * tokens :]
    ).astype(jnp.bfloat16)

    for k in range(1, ne):
        a2a_copy(k).wait_send()
    for j in range(1, nd):
        for s in range(nt):
            for c in range(CHUNKS):
                y_copy(j, d, s, c).wait_send()
    z_drain(0, own)

    def drain(j, carry):
        b = lax.rem(d + j, nd)
        z_drain(1 + j, acts.at[b])
        for k in range(1, ne):
            return_copy(j, b, k).wait_send()

        @pl.when(j > 0)
        def _():
            return_copy(j, b, 0).wait_send()

        return carry

    lax.fori_loop(0, nd, drain, 0)


def body(mesh, hidden_states, chosen_experts, choice_weights, gate_proj, up_proj, down_proj):
    nd, ne, nt = mesh.shape["dp"], mesh.shape["expert"], mesh.shape["tensor"]
    tokens, width = hidden_states.shape
    units = gate_proj.shape[2]
    slots = ne * CAP
    vmem = pl.BlockSpec(memory_space=pltpu.VMEM)
    hbm = pl.BlockSpec(memory_space=pl.ANY)
    bf16, f32, dma = jnp.bfloat16, jnp.float32, pltpu.SemaphoreType.DMA
    lots = (nt + HOP - 1) // HOP
    return pl.pallas_call(
        functools.partial(kernel, nd, ne, nt),
        out_shape=jax.ShapeDtypeStruct((tokens, width), bf16),
        in_specs=[vmem, vmem, vmem, hbm, hbm, hbm],
        out_specs=vmem,
        scratch_shapes=[
            pltpu.VMEM((ne, CAP, width), bf16),
            pltpu.VMEM((nd, nt, ne, CAP, width), bf16),
            pltpu.VMEM((nd, nt, ne, CAP, units), bf16),
            pltpu.VMEM((nt, width, units), bf16),
            pltpu.VMEM((nt, width, units), bf16),
            pltpu.VMEM((nt, units, width), bf16),
            pltpu.VMEM((slots, units), f32),
            pltpu.VMEM((slots, units), f32),
            pltpu.VMEM((slots, width), f32),
            pltpu.VMEM((nd, ne, CAP, width), bf16),
            pltpu.VMEM((nd, ne, CAP, width), bf16),
            pltpu.VMEM((3 * tokens, slots), bf16),
            dma((3, nt)),
            dma((ne,)),
            dma((ne,)),
            dma((1 + nd, CHUNKS, 2, lots, HOP)),
            dma((1 + nd, CHUNKS, nt)),
            dma((nd, nt, CHUNKS)),
            dma((nd, nt, CHUNKS)),
            dma((nd, ne)),
            dma((nd, ne)),
        ],
        compiler_params=pltpu.CompilerParams(
            collective_id=0, has_side_effects=True, vmem_limit_bytes=48 << 20
        ),
        name="experts",
    )(hidden_states, chosen_experts, choice_weights, gate_proj, up_proj, down_proj)


def solution(mesh):
    in_specs = (
        P(("dp", "expert"), "tensor"),
        P(("dp", "expert"), None),
        P(("dp", "expert"), None),
        P("expert", None, ("dp", "tensor")),
        P("expert", None, ("dp", "tensor")),
        P("expert", "dp", "tensor"),
    )
    out_specs = P(("dp", "expert"), "tensor")
    return jax.shard_map(
        functools.partial(body, mesh), mesh=mesh, in_specs=in_specs, out_specs=out_specs,
        check_vma=False,
    )
```

time: 132 us -> 54.3 us (0.41)
  waiting for transfers between devices: 69.2 us -> 0 us
  Pallas kernels: 0 us -> 51.1 us
  blocking collectives: 24.9 us -> 0 us
  matrix products: 17.4 us -> 0 us
  between operations: 13.2 us -> 0.01 us
  starting transfers between devices: 3.41 us -> 0 us
  other arithmetic: 2.66 us -> 0 us
  local copies, waits for them, and re-layouts: 1.1 us -> 2.99 us
    pallas_call x0 -> x1, Pallas kernels: none -> 51.1 us  [body(): pl.pallas_call(functools.partial(kernel, nd, ne, nt), out_shape=jax.Shape...]
    all_gather x2 -> x0, waiting for transfers between devices: 50.4 us -> none  [the longest x1 28 us: body(): unit_rows = lax.all_gather(activated, 'tensor', axis=1, tiled=True)]
    dot_general x5 -> x0, matrix products: 17.4 us -> none  [the longest x1 5.79 us: body(): jnp.dot(unit_rows, down_weights, preferred_element_type=jnp.float32)]
    all_gather x1 -> x0, blocking collectives: 16.2 us -> none  [body(): features = lax.all_gather(arrived, 'tensor', axis=1, tiled=True)]
    reduce_scatter x1 -> x0, waiting for transfers between devices: 14.2 us -> none  [body(): lax.psum_scatter(jnp.dot(unit_rows, down_weights, preferred_element_type=...]
    all_to_all x1 -> x0, blocking collectives: 8.64 us -> none  [body(): lax.all_to_all(packed, 'expert', split_axis=0, concat_axis=0, tiled=True)]
    all_to_all x1 -> x0, waiting for transfers between devices: 4.58 us -> none  [body(): lax.all_to_all(outgoing, 'expert', split_axis=0, concat_axis=0, tiled=True)]
    all_to_all x1 -> x0, starting transfers between devices: 3.32 us -> none  [body(): lax.all_to_all(outgoing, 'expert', split_axis=0, concat_axis=0, tiled=True)]
  transfers between devices with their start and end apart: 4 -> 0, of which waited for: 4 -> 0; matrix products, arithmetic and copies ran while one was open for 0% -> 0% of each run, Pallas kernels for 0% -> 0%
where the time goes in v1:
time: 54.3 us; the launch traced here: 54.1 us
  Pallas kernels  51.1 us (94%)
  local copies, waits for them, and re-layouts  2.99 us (6%)
    pallas_call x1, Pallas kernels, body(): pl.pallas_call(functools.partial(kernel, nd, ne, nt), out_shape=jax.Shape...  51.1 us
    unnamed x5, local copies, waits for them, and re-layouts  2.99 us

profile of v1, /device:TPU:0, one launch (start us, length us, event | category | flops | bytes accessed | tf_op | source)
XLA Modules:
  0.0 54.1 jit_solution(9185969654196640490)
XLA Ops:
  0.0 0.8 %copy.7.ids_ref = s32[32,2]{1,0:T(8,128)S(1)} copy(s32[32,2]{0,1:T(2,128)} %param.7) | data formatting | bytes 512 | tf_op args[1]
  0.8 0.8 %copy.8.weights_ref = f32[32,2]{1,0:T(8,128)S(1)} copy(f32[32,2]{0,1:T(2,128)} %param.8) | data formatting | bytes 512 | tf_op args[2]
  1.5 0.0 copy-start
  1.5 0.8 %copy-done = bf16[32,1024]{1,0:T(8,128)(2,1)S(1)} copy-done((bf16[32,1024]{1,0:T(8,128)(2,1)S(1)}, bf16[32,1024]{1,0:T(8,128)(2,1)}, u32[]{:S(2)}) %copy-start) | copy-done | bytes 65560
  2.4 51.1 %experts.1 = bf16[32,1024]{1,0:T(8,128)(2,1)S(1)} custom-call(bf16[32,1024]{1,0:T(8,128)(2,1)S(1)} %copy-done, s32[32,2]{1,0:T(8,128)S(1)} %copy.7.ids_ref, f32[32,2]{1,0:T(8,128)S(1)} %copy.8.weights_ref, bf16[1,4096,1024]{2,1,0:T(8,128)(2,1)} %gate_hbm.1, bf16[1,4096,1024]{2,1,0:T(8,128)(2,1)} %up_hbm.1, bf16[1,4096,1024]{2,1,0:T(8,128)(2,1)} %down_hbm.1), custom_call_target="tpu_custom_call" | custom-call | tf_op jit(solution)/shard_map/experts/pallas_call | solution.py:367
  53.5 0.6 %copy.10 = bf16[32,1024]{1,0:T(8,128)(2,1)} copy(bf16[32,1024]{1,0:T(8,128)(2,1)S(1)} %experts.1) | data formatting | bytes 131072
Async XLA Ops:
  1.5 0.8 %copy-start = (bf16[32,1024]{1,0:T(8,128)(2,1)S(1)}, bf16[32,1024]{1,0:T(8,128)(2,1)}, u32[]{:S(2)}) copy-start(bf16[32,1024]{1,0:T(8,128)(2,1)} %hidden_ref.1) | copy-start | bytes 196612

commit v2 on v1

v2 whole, which is shorter than its diff:
```python
import functools

import jax
import jax.numpy as jnp
from jax import lax
from jax.experimental import pallas as pl
from jax.experimental.pallas import tpu as pltpu
from jax.sharding import PartitionSpec as P

CAP = 16
TOKEN_HOP = 2
UNIT_HOP = 1
CHUNKS = 2
TILE = 1024
MESH = pl.DeviceIdType.MESH


def kernel(
    nd, ne, nt,
    hidden_hbm, ids_hbm, weights_hbm, gate_hbm, up_hbm, down_hbm, out_ref,
    tokens_in, ids_ref, weights_ref, packed, feats, acts, gate_w, up_w, down_w,
    gate_acc, up_acc, down_acc, outgoing, returned, table,
    in_sem, w_sem, x_send, x_recv, z_send, z_recv, u_send, u_recv,
    y_send, y_recv, ret_send, ret_recv,
):
    d, e, t = lax.axis_index("dp"), lax.axis_index("expert"), lax.axis_index("tensor")
    tokens, width = tokens_in.shape[1:]
    slots = ne * CAP
    units = gate_w.shape[2]
    part = ne // CHUNKS
    tile_u = min(TILE, units)
    tile_f = min(TILE, width)

    barrier = pltpu.get_barrier_semaphore()
    for j in range(nd):
        for k in range(ne):
            if j or k:
                pl.semaphore_signal(
                    barrier, inc=1, device_id_type=MESH,
                    device_id=(lax.rem(d + j, nd), lax.rem(e + k, ne), t),
                )
    for k in range(1, nt):
        pl.semaphore_signal(
            barrier, inc=1, device_id=(d, e, lax.rem(t + k, nt)), device_id_type=MESH
        )
    inputs = (
        pltpu.make_async_copy(ids_hbm, ids_ref, in_sem.at[0]),
        pltpu.make_async_copy(weights_hbm, weights_ref, in_sem.at[1]),
        pltpu.make_async_copy(hidden_hbm, tokens_in.at[t], in_sem.at[2]),
    )
    for copy in inputs:
        copy.start()

    def weight_copy(i, s):
        size = units if i == 2 else width
        source = (gate_hbm, up_hbm, down_hbm)[i]
        return pltpu.make_async_copy(
            source.at[0, pl.ds(pl.multiple_of(s * size, size), size)],
            (gate_w, up_w, down_w)[i].at[s],
            w_sem.at[i, s],
        )

    order = [0]
    for k in range(1, nt):
        order.append((k + 1) // 2 if k % 2 else nt - k // 2)
    for k in order:
        weight_copy(0, lax.rem(t + k, nt)).start()
        weight_copy(1, lax.rem(t + k, nt)).start()
    for k in order:
        weight_copy(2, lax.rem(t + k, nt)).start()

    for copy in inputs:
        copy.wait()
    slot = lax.broadcasted_iota(jnp.int32, (slots, tokens), 0)
    slot_expert = lax.shift_right_logical(slot, CAP.bit_length() - 1)
    slot_place = slot - slot_expert * CAP
    named = jnp.zeros((slots, tokens), jnp.float32)
    weighted = jnp.zeros((slots, tokens), jnp.float32)
    for row in range(ids_ref.shape[0]):
        match = ids_ref[row : row + 1, :] == slot_expert
        named = jnp.where(match, 1.0, named)
        weighted = jnp.where(match, weights_ref[row : row + 1, :], weighted)
    earlier = lax.broadcasted_iota(jnp.int32, (tokens, tokens), 0) < (
        lax.broadcasted_iota(jnp.int32, (tokens, tokens), 1)
    )
    position = jnp.dot(
        named.astype(jnp.bfloat16),
        jnp.where(earlier, 1.0, 0.0).astype(jnp.bfloat16),
        preferred_element_type=jnp.float32,
    )
    placing = jnp.where(position == slot_place.astype(jnp.float32), named, 0.0)
    weighted = weighted * placing
    placing = placing.astype(jnp.bfloat16)
    high = weighted.astype(jnp.bfloat16)
    rest = weighted - high.astype(jnp.float32)
    middle = rest.astype(jnp.bfloat16)
    table[0] = high
    table[1] = middle
    table[2] = (rest - middle.astype(jnp.float32)).astype(jnp.bfloat16)
    table[3] = placing

    def x_copy(s, k):
        return pltpu.make_async_remote_copy(
            src_ref=packed.at[s, lax.rem(e + k, ne)],
            dst_ref=feats.at[d, s, e],
            send_sem=x_send.at[s, k],
            recv_sem=x_recv.at[s, e],
            device_id=(d, lax.rem(e + k, ne), t),
            device_id_type=MESH,
        )

    def x_spread(s):
        packed[s] = (
            jnp.dot(table[3], tokens_in[s], preferred_element_type=jnp.float32)
            .astype(jnp.bfloat16)
            .reshape(ne, CAP, width)
        )
        for k in range(1, ne):
            x_copy(s, k).start()
        feats[d, s, e] = packed[s, e]

    def x_arrive(s):
        for k in range(1, ne):
            source = lax.rem(e + k, ne)
            pltpu.make_async_remote_copy(
                src_ref=packed.at[s, source],
                dst_ref=feats.at[d, s, source],
                send_sem=x_send.at[s, k],
                recv_sem=x_recv.at[s, source],
                device_id=(d, source, t),
                device_id_type=MESH,
            ).wait_recv()

    class Line:
        def __init__(self, hop, chunks, block, send_sem, recv_sem):
            self.hop, self.chunks, self.block = hop, chunks, block
            self.send_sem, self.recv_sem = send_sem, recv_sem

        def copy(self, s, c, side, dist, hop):
            block = self.block(s, c)
            return pltpu.make_async_remote_copy(
                src_ref=block,
                dst_ref=block,
                send_sem=self.send_sem(c, side, dist // self.hop, hop - 1),
                recv_sem=self.recv_sem(c, s),
                device_id=(d, e, t + hop * (1 - 2 * side)),
                device_id_type=MESH,
            )

        def targets(self, side, dist, act):
            step = 1 - 2 * side
            s = t - step * dist
            for hop in range(1, self.hop + 1):
                to = t + step * hop

                @pl.when((s >= 0) & (s < nt) & (to >= 0) & (to < nt))
                def _():
                    act(s, hop)

        def forward(self, side, dist, c):
            if dist % self.hop == 0:
                self.targets(
                    side, dist, lambda s, hop: self.copy(s, c, side, dist, hop).start()
                )

        def send_own(self):
            for c in range(self.chunks):
                for side in range(2):
                    self.forward(side, 0, c)

        def arrive(self, side, dist, s):
            for c in range(self.chunks):
                self.copy(s, c, 0, 0, 1).wait_recv()
                self.forward(side, dist, c)

        def drain(self):
            for c in range(self.chunks):
                for side in range(2):
                    for dist in range(0, nt, self.hop):
                        self.targets(
                            side, dist,
                            lambda s, hop: self.copy(s, c, side, dist, hop).wait_send(),
                        )

    token_line = Line(
        TOKEN_HOP, 1, lambda s, c: tokens_in.at[s],
        lambda c, side, i, h: z_send.at[side, i, h], lambda c, s: z_recv.at[s],
    )

    def unit_line(j, b):
        return Line(
            UNIT_HOP, CHUNKS, lambda s, c: acts.at[b, s, pl.ds(c * part, part)],
            lambda c, side, i, h: u_send.at[j, c, side, i, h],
            lambda c, s: u_recv.at[j, c, s],
        )

    def y_copy(j, b, s, c):
        block = feats.at[b, s, pl.ds(c * part, part)]
        return pltpu.make_async_remote_copy(
            src_ref=block,
            dst_ref=block,
            send_sem=y_send.at[j, s, c],
            recv_sem=y_recv.at[b, s, c],
            device_id=(lax.rem(d + j, nd), e, t),
            device_id_type=MESH,
        )

    def y_spread(s, c):
        for j in range(1, nd):
            y_copy(j, d, s, c).start()

    def gate_up(b, s, first):
        @pl.loop(0, units // tile_u)
        def _(i):
            columns = pl.ds(pl.multiple_of(i * tile_u, tile_u), tile_u)
            rows = feats[b, s].reshape(slots, width)
            gate = jnp.dot(rows, gate_w[s, :, columns], preferred_element_type=jnp.float32)
            up = jnp.dot(rows, up_w[s, :, columns], preferred_element_type=jnp.float32)
            if first is True:
                gate_acc[:, columns] = gate
                up_acc[:, columns] = up
            else:
                gate_acc[:, columns] += gate
                up_acc[:, columns] += up

    def activate(b):
        @pl.loop(0, units // tile_u)
        def _(i):
            columns = pl.ds(pl.multiple_of(i * tile_u, tile_u), tile_u)
            gate = gate_acc[:, columns]
            value = gate / (1.0 + jnp.exp(-gate)) * up_acc[:, columns]
            acts[b, t, :, :, columns] = value.astype(jnp.bfloat16).reshape(ne, CAP, tile_u)

    def down(b, s, first):
        @pl.loop(0, width // tile_f)
        def _(i):
            columns = pl.ds(pl.multiple_of(i * tile_f, tile_f), tile_f)
            rows = acts[b, s].reshape(slots, units)
            value = jnp.dot(rows, down_w[s, :, columns], preferred_element_type=jnp.float32)
            if first:
                down_acc[:, columns] = value
            else:
                down_acc[:, columns] += value

    def at_distance(dist, act):
        for side in range(2):
            s = t - (1 - 2 * side) * dist

            @pl.when((s >= 0) & (s < nt))
            def _():
                act(side, s)

    pl.semaphore_wait(barrier, nd * ne + nt - 2)
    token_line.send_own()
    x_spread(t)

    def use(s, first):
        x_arrive(s)
        for c in range(CHUNKS):
            y_spread(s, c)
        weight_copy(0, s).wait()
        weight_copy(1, s).wait()
        gate_up(d, s, first)

    for dist in range(1, nt + 1):
        if dist < nt:
            def take(side, s):
                token_line.arrive(side, dist, s)
                x_spread(s)

            at_distance(dist, take)
        if dist == 1:
            use(t, True)
        else:
            at_distance(dist - 1, lambda side, s: use(s, False))
    activate(d)
    unit_line(0, d).send_own()

    def other_rows(j, carry):
        b = lax.rem(d + j, nd)

        def arrive(s):
            for c in range(CHUNKS):
                y_copy(j, b, s, c).wait_recv()

        arrive(t)
        gate_up(b, t, True)

        def shard(k, carry):
            s = lax.rem(t + k, nt)
            arrive(s)
            gate_up(b, s, False)
            return carry

        lax.fori_loop(1, nt, shard, 0)
        activate(b)
        unit_line(j, b).send_own()
        return carry

    lax.fori_loop(1, nd, other_rows, 0)

    for k in range(nt):
        weight_copy(2, lax.rem(t + k, nt)).wait()

    def return_copy(j, b, k):
        to = lax.rem(e + k, ne)
        return pltpu.make_async_remote_copy(
            src_ref=outgoing.at[b, to],
            dst_ref=returned.at[d, e],
            send_sem=ret_send.at[j, k],
            recv_sem=ret_recv.at[d, e],
            device_id=(b, to, t),
            device_id_type=MESH,
        )

    def finish(j, carry):
        b = lax.rem(d + j, nd)
        line = unit_line(j, b)
        down(b, t, True)
        for dist in range(1, nt):
            at_distance(dist, lambda side, s: line.arrive(side, dist, s))
            at_distance(dist, lambda side, s: down(b, s, False))
        outgoing[b] = down_acc[...].astype(jnp.bfloat16).reshape(ne, CAP, width)
        for k in range(1, ne):
            return_copy(j, b, k).start()

        @pl.when(j == 0)
        def _():
            returned[d, e] = outgoing[d, e]

        @pl.when(j > 0)
        def _():
            return_copy(j, b, 0).start()

        return carry

    lax.fori_loop(0, nd, finish, 0)

    for j in range(nd):
        for k in range(ne):
            if j or k:
                b, source = lax.rem(d + j, nd), lax.rem(e + k, ne)
                pltpu.make_async_remote_copy(
                    src_ref=outgoing.at[0, 0],
                    dst_ref=returned.at[b, source],
                    send_sem=ret_send.at[j, k],
                    recv_sem=ret_recv.at[b, source],
                    device_id=(b, source, t),
                    device_id_type=MESH,
                ).wait_recv()
    total = jnp.zeros((tokens, width), jnp.float32)
    for b in range(nd):
        rows = returned[b].reshape(slots, width)
        for i in range(3):
            total += lax.dot_general(
                table[i], rows, (((0,), (0,)), ((), ())), preferred_element_type=jnp.float32
            )
    out_ref[...] = total.astype(jnp.bfloat16)

    for s in range(nt):
        for k in range(1, ne):
            x_copy(s, k).wait_send()
    for j in range(1, nd):
        for s in range(nt):
            for c in range(CHUNKS):
                y_copy(j, d, s, c).wait_send()
    token_line.drain()

    def drain(j, carry):
        b = lax.rem(d + j, nd)
        unit_line(j, b).drain()
        for k in range(1, ne):
            return_copy(j, b, k).wait_send()

        @pl.when(j > 0)
        def _():
            return_copy(j, b, 0).wait_send()

        return carry

    lax.fori_loop(0, nd, drain, 0)


def body(mesh, hidden_states, chosen_experts, choice_weights, gate_proj, up_proj, down_proj):
    nd, ne, nt = mesh.shape["dp"], mesh.shape["expert"], mesh.shape["tensor"]
    tokens, width = hidden_states.shape
    units = gate_proj.shape[2]
    slots = ne * CAP
    vmem = pl.BlockSpec(memory_space=pltpu.VMEM)
    hbm = pl.BlockSpec(memory_space=pl.ANY)
    bf16, f32, dma = jnp.bfloat16, jnp.float32, pltpu.SemaphoreType.DMA
    token_sends = (2, pl.cdiv(nt, TOKEN_HOP), TOKEN_HOP)
    unit_sends = (nd, CHUNKS, 2, pl.cdiv(nt, UNIT_HOP), UNIT_HOP)
    return pl.pallas_call(
        functools.partial(kernel, nd, ne, nt),
        out_shape=jax.ShapeDtypeStruct((tokens, width), bf16),
        in_specs=[hbm] * 6,
        out_specs=vmem,
        scratch_shapes=[
            pltpu.VMEM((nt, tokens, width), bf16),
            pltpu.VMEM(chosen_experts.shape[::-1], jnp.int32),
            pltpu.VMEM(choice_weights.shape[::-1], f32),
            pltpu.VMEM((nt, ne, CAP, width), bf16),
            pltpu.VMEM((nd, nt, ne, CAP, width), bf16),
            pltpu.VMEM((nd, nt, ne, CAP, units), bf16),
            pltpu.VMEM((nt, width, units), bf16),
            pltpu.VMEM((nt, width, units), bf16),
            pltpu.VMEM((nt, units, width), bf16),
            pltpu.VMEM((slots, units), f32),
            pltpu.VMEM((slots, units), f32),
            pltpu.VMEM((slots, width), f32),
            pltpu.VMEM((nd, ne, CAP, width), bf16),
            pltpu.VMEM((nd, ne, CAP, width), bf16),
            pltpu.VMEM((4, slots, tokens), bf16),
            dma((3,)),
            dma((3, nt)),
            dma((nt, ne)),
            dma((nt, ne)),
            dma(token_sends),
            dma((nt,)),
            dma(unit_sends),
            dma((nd, CHUNKS, nt)),
            dma((nd, nt, CHUNKS)),
            dma((nd, nt, CHUNKS)),
            dma((nd, ne)),
            dma((nd, ne)),
        ],
        compiler_params=pltpu.CompilerParams(
            collective_id=0, has_side_effects=True, vmem_limit_bytes=48 << 20
        ),
        name="experts",
    )(hidden_states, chosen_experts.T, choice_weights.T, gate_proj, up_proj, down_proj)


def solution(mesh):
    in_specs = (
        P(("dp", "expert"), "tensor"),
        P(("dp", "expert"), None),
        P(("dp", "expert"), None),
        P("expert", None, ("dp", "tensor")),
        P("expert", None, ("dp", "tensor")),
        P("expert", "dp", "tensor"),
    )
    out_specs = P(("dp", "expert"), "tensor")
    return jax.shard_map(
        functools.partial(body, mesh), mesh=mesh, in_specs=in_specs, out_specs=out_specs,
        check_vma=False,
    )
```

time: 54.3 us -> 50.5 us (0.930)
  Pallas kernels: 51.1 us -> 47.4 us
    pallas_call x1, Pallas kernels: 51.1 us -> 47.4 us  [body(): pl.pallas_call(functools.partial(kernel, nd, ne, nt), out_shape=jax.Shape...]
    unnamed x5 -> x7, local copies, waits for them, and re-layouts: 2.99 us -> 2.83 us
where the time goes in v2:
time: 50.5 us; the launch traced here: 50.3 us
  Pallas kernels  47.4 us (94%)
  local copies, waits for them, and re-layouts  2.83 us (6%)
    pallas_call x1, Pallas kernels, body(): pl.pallas_call(functools.partial(kernel, nd, ne, nt), out_shape=jax.Shape...  47.4 us
    unnamed x7, local copies, waits for them, and re-layouts  2.83 us

profile of v2, /device:TPU:0, one launch (start us, length us, event | category | flops | bytes accessed | tf_op | source)
XLA Modules:
  0.0 50.3 jit_solution(1785621645924434078)
XLA Ops:
  0.0 0.0 copy-start
  0.0 0.8 %copy-done = bf16[32,1024]{1,0:T(8,128)(2,1)S(1)} copy-done((bf16[32,1024]{1,0:T(8,128)(2,1)S(1)}, bf16[32,1024]{1,0:T(8,128)(2,1)}, u32[]{:S(2)}) %copy-start) | copy-done | bytes 65560
  0.8 0.0 copy-start.1
  0.8 0.7 %copy-done.1 = s32[32,2]{0,1:T(2,128)S(1)} copy-done((s32[32,2]{0,1:T(2,128)S(1)}, s32[32,2]{0,1:T(2,128)}, u32[]{:S(2)}) %copy-start.1) | copy-done | bytes 280
  1.5 0.0 copy-start.2
  1.5 0.7 %copy-done.2 = f32[32,2]{0,1:T(2,128)S(1)} copy-done((f32[32,2]{0,1:T(2,128)S(1)}, f32[32,2]{0,1:T(2,128)}, u32[]{:S(2)}) %copy-start.2) | copy-done | bytes 280
  2.2 47.4 %experts.1 = bf16[32,1024]{1,0:T(8,128)(2,1)S(1)} custom-call(bf16[32,1024]{1,0:T(8,128)(2,1)S(1)} %copy-done, s32[2,32]{1,0:T(2,128)S(1)} %bitcast.2, f32[2,32]{1,0:T(2,128)S(1)} %bitcast.3, bf16[1,4096,1024]{2,1,0:T(8,128)(2,1)} %gate_hbm.1, bf16[1,4096,1024]{2,1,0:T(8,128)(2,1)} %up_hbm.1, bf16[1,4096,1024]{2,1,0:T(8,128)(2,1)} %down_hbm.1), custom_call_target="tpu_custom_call" | custom-call | tf_op jit(solution)/shard_map/experts/pallas_call | solution.py:394
  49.7 0.6 %copy.8 = bf16[32,1024]{1,0:T(8,128)(2,1)} copy(bf16[32,1024]{1,0:T(8,128)(2,1)S(1)} %experts.1) | data formatting | bytes 131072
Async XLA Ops:
  0.0 0.8 %copy-start = (bf16[32,1024]{1,0:T(8,128)(2,1)S(1)}, bf16[32,1024]{1,0:T(8,128)(2,1)}, u32[]{:S(2)}) copy-start(bf16[32,1024]{1,0:T(8,128)(2,1)} %hidden_hbm.1) | copy-start | bytes 196612
  0.8 0.7 %copy-start.1 = (s32[32,2]{0,1:T(2,128)S(1)}, s32[32,2]{0,1:T(2,128)}, u32[]{:S(2)}) copy-start(s32[32,2]{0,1:T(2,128)} %param.7) | copy-start | bytes 772
  1.5 0.7 %copy-start.2 = (f32[32,2]{0,1:T(2,128)S(1)}, f32[32,2]{0,1:T(2,128)}, u32[]{:S(2)}) copy-start(f32[32,2]{0,1:T(2,128)} %param.8) | copy-start | bytes 772

commit v3 on v2

--- a/solution.py
+++ b/solution.py
@@ -8,8 +8,8 @@
 from jax.sharding import PartitionSpec as P
 
 CAP = 16
-TOKEN_HOP = 2
-UNIT_HOP = 1
+TOKEN_HOP = 1
+UNIT_HOP = 2
 CHUNKS = 2
 TILE = 1024
 MESH = pl.DeviceIdType.MESH
@@ -276,32 +276,6 @@
     activate(d)
     unit_line(0, d).send_own()
 
-    def other_rows(j, carry):
-        b = lax.rem(d + j, nd)
-
-        def arrive(s):
-            for c in range(CHUNKS):
-                y_copy(j, b, s, c).wait_recv()
-
-        arrive(t)
-        gate_up(b, t, True)
-
-        def shard(k, carry):
-            s = lax.rem(t + k, nt)
-            arrive(s)
-            gate_up(b, s, False)
-            return carry
-
-        lax.fori_loop(1, nt, shard, 0)
-        activate(b)
-        unit_line(j, b).send_own()
-        return carry
-
-    lax.fori_loop(1, nd, other_rows, 0)
-
-    for k in range(nt):
-        weight_copy(2, lax.rem(t + k, nt)).wait()
-
     def return_copy(j, b, k):
         to = lax.rem(e + k, ne)
         return pltpu.make_async_remote_copy(
@@ -313,13 +287,7 @@
             device_id_type=MESH,
         )
 
-    def finish(j, carry):
-        b = lax.rem(d + j, nd)
-        line = unit_line(j, b)
-        down(b, t, True)
-        for dist in range(1, nt):
-            at_distance(dist, lambda side, s: line.arrive(side, dist, s))
-            at_distance(dist, lambda side, s: down(b, s, False))
+    def finish(j, b):
         outgoing[b] = down_acc[...].astype(jnp.bfloat16).reshape(ne, CAP, width)
         for k in range(1, ne):
             return_copy(j, b, k).start()
@@ -332,9 +300,44 @@
         def _():
             return_copy(j, b, 0).start()
 
+    def step(j, carry):
+        b, before = lax.rem(d + j, nd), lax.rem(d + j - 1, nd)
+        line = unit_line(j - 1, before)
+
+        def pass_on(dist):
+            at_distance(dist, lambda side, s: line.arrive(side, dist, s))
+
+        for k in range(nt):
+            s = lax.rem(t + order[k], nt)
+            for c in range(CHUNKS):
+                y_copy(j, b, s, c).wait_recv()
+            gate_up(b, s, k == 0)
+            if 0 < k < nt - 1:
+                pass_on(k)
+        activate(b)
+        unit_line(j, b).send_own()
+
+        @pl.when(j == 1)
+        def _():
+            for k in range(nt):
+                weight_copy(2, lax.rem(t + k, nt)).wait()
+
+        down(before, t, True)
+        for dist in range(1, nt):
+            if dist == nt - 1:
+                pass_on(dist)
+            at_distance(dist, lambda side, s: down(before, s, False))
+        finish(j - 1, before)
         return carry
 
-    lax.fori_loop(0, nd, finish, 0)
+    lax.fori_loop(1, nd, step, 0)
+    last = lax.rem(d + nd - 1, nd)
+    line = unit_line(nd - 1, last)
+    down(last, t, True)
+    for dist in range(1, nt):
+        at_distance(dist, lambda side, s: line.arrive(side, dist, s))
+        at_distance(dist, lambda side, s: down(last, s, False))
+    finish(nd - 1, last)
 
     for j in range(nd):
         for k in range(ne):

time: 50.5 us -> 51.9 us (1.028)
  Pallas kernels: 47.4 us -> 48.9 us
    pallas_call x1, Pallas kernels: 47.4 us -> 48.9 us  [body(): pl.pallas_call(functools.partial(kernel, nd, ne, nt), out_shape=jax.Shape...]
where the time goes in v3:
time: 51.9 us; the launch traced here: 51.7 us
  Pallas kernels  48.9 us (94%)
  local copies, waits for them, and re-layouts  2.83 us (5%)
    pallas_call x1, Pallas kernels, body(): pl.pallas_call(functools.partial(kernel, nd, ne, nt), out_shape=jax.Shape...  48.9 us
    unnamed x7, local copies, waits for them, and re-layouts  2.83 us

profile of v3, /device:TPU:0, one launch (start us, length us, event | category | flops | bytes accessed | tf_op | source)
XLA Modules:
  0.0 51.7 jit_solution(16436859054840568673)
XLA Ops:
  0.0 0.0 copy-start
  0.0 0.8 %copy-done = bf16[32,1024]{1,0:T(8,128)(2,1)S(1)} copy-done((bf16[32,1024]{1,0:T(8,128)(2,1)S(1)}, bf16[32,1024]{1,0:T(8,128)(2,1)}, u32[]{:S(2)}) %copy-start) | copy-done | bytes 65560
  0.8 0.0 copy-start.1
  0.8 0.7 %copy-done.1 = s32[32,2]{0,1:T(2,128)S(1)} copy-done((s32[32,2]{0,1:T(2,128)S(1)}, s32[32,2]{0,1:T(2,128)}, u32[]{:S(2)}) %copy-start.1) | copy-done | bytes 280
  1.5 0.0 copy-start.2
  1.5 0.7 %copy-done.2 = f32[32,2]{0,1:T(2,128)S(1)} copy-done((f32[32,2]{0,1:T(2,128)S(1)}, f32[32,2]{0,1:T(2,128)}, u32[]{:S(2)}) %copy-start.2) | copy-done | bytes 280
  2.2 48.9 %experts.1 = bf16[32,1024]{1,0:T(8,128)(2,1)S(1)} custom-call(bf16[32,1024]{1,0:T(8,128)(2,1)S(1)} %copy-done, s32[2,32]{1,0:T(2,128)S(1)} %bitcast.2, f32[2,32]{1,0:T(2,128)S(1)} %bitcast.3, bf16[1,4096,1024]{2,1,0:T(8,128)(2,1)} %gate_hbm.1, bf16[1,4096,1024]{2,1,0:T(8,128)(2,1)} %up_hbm.1, bf16[1,4096,1024]{2,1,0:T(8,128)(2,1)} %down_hbm.1), custom_call_target="tpu_custom_call" | custom-call | tf_op jit(solution)/shard_map/experts/pallas_call | solution.py:397
  51.1 0.6 %copy.8 = bf16[32,1024]{1,0:T(8,128)(2,1)} copy(bf16[32,1024]{1,0:T(8,128)(2,1)S(1)} %experts.1) | data formatting | bytes 131072
Async XLA Ops:
  0.0 0.8 %copy-start = (bf16[32,1024]{1,0:T(8,128)(2,1)S(1)}, bf16[32,1024]{1,0:T(8,128)(2,1)}, u32[]{:S(2)}) copy-start(bf16[32,1024]{1,0:T(8,128)(2,1)} %hidden_hbm.1) | copy-start | bytes 196612
  0.8 0.7 %copy-start.1 = (s32[32,2]{0,1:T(2,128)S(1)}, s32[32,2]{0,1:T(2,128)}, u32[]{:S(2)}) copy-start(s32[32,2]{0,1:T(2,128)} %param.7) | copy-start | bytes 772
  1.5 0.7 %copy-start.2 = (f32[32,2]{0,1:T(2,128)S(1)}, f32[32,2]{0,1:T(2,128)}, u32[]{:S(2)}) copy-start(f32[32,2]{0,1:T(2,128)} %param.8) | copy-start | bytes 772
